TPU v7x, 512 devices: a whole 4x4x16 slice. The times are simulated.
512 devices in a mesh: dp: 16 (over z_hi, x), shard: 32 (over y, z_lo, core).
Axes of the slice: x: 4, y: 4, z: 16 (z_hi: 4, z_lo: 4; z = z_hi * 4 + z_lo), core: 2. Of those that a mesh axis runs over, the one named last changes fastest.
Arguments:
- inputs: bfloat16 [2, 4096, 8192], P(None, 'dp', 'shard'), may hold values from -6 to 6
- key_panel: bfloat16 [8192, 4096], P('dp', 'shard'), may hold values from -0.0625 to 0.0625
- value_panel: bfloat16 [8192, 4096], P('dp', 'shard'), may hold values from -0.0625 to 0.0625
- short_filters: float32 [2, 4096, 7], P(None, 'shard'), may hold values from -2 to 2
- medium_filters: float32 [256, 128], P('shard'), may hold values from -0.5 to 0.5
- lengths: int32 [2], replicated, may hold values from 2048 to 4096, as said below
- cotangent: bfloat16 [2, 4096, 4096], P(None, 'dp', 'shard'), may hold values from -0.099609375 to 0.099609375
Outputs:
- mixed: bfloat16 [2, 4096, 4096], P(None, 'dp', 'shard')
- key_grad: bfloat16 [8192, 4096], P('dp', 'shard')
- value_grad: bfloat16 [8192, 4096], P('dp', 'shard')
- short_grad: float32 [2, 4096, 7], P(None, 'shard')
- medium_grad: float32 [256, 128], P('shard')
Inputs may be any that keep to these rules, and one draw needn't show every extreme that they name: `lengths`: each length is a multiple of 16; one window in every draw has the full length 4096, the others are shorter.
All inputs are finite; a program needn't handle non-finite values.
Results may differ from a plain program's by a relative error of at most 0.014.
Values may be sent and summed in bfloat16 or wider, within the bound.
No kernel may reach another device: no remote copies, remote signals or barrier semaphores. Data moves between devices by JAX's collectives and lax.ppermute only.
A program may use at most 64 MiB of HBM per device.

v0:
```python
import jax
import jax.numpy as jnp
from jax import lax
from jax.sharding import PartitionSpec as P


def shifted(value, axis, steps):
    count = lax.axis_size(axis)
    first, last = (max(0, -steps), min(count, count - steps))
    return lax.ppermute(value, axis, [(source, source + steps) for source in range(first, last)])


def band(filters, count):
    groups, taps = filters.shape
    width = count + taps - 1
    padded = jnp.concatenate([filters, jnp.zeros((groups, count), jnp.float32)], axis=1)
    tiled = jnp.tile(padded, (1, count))[:, : count * width]
    return tiled.reshape(groups, count, width)


def band_sums(correlation, count, taps):
    groups, _, width = correlation.shape
    flat = correlation.reshape(groups, count * width)
    padded = jnp.concatenate([flat, jnp.zeros((groups, count), jnp.float32)], axis=1)
    skewed = padded.reshape(groups, count, width + 1)
    return jnp.sum(skewed, axis=1)[:, :taps][:, ::-1]


def short_taps(extended, filters, count):
    width = filters.shape[-1]
    total = jnp.zeros(extended.shape[:2] + (count, extended.shape[3]), jnp.float32)
    for tap in range(width):
        begin = width - 1 - tap
        total = total + filters[:, None, None, :, tap] * extended[
            :, :, begin : begin + count
        ].astype(jnp.float32)
    return total


def short_ahead(extended, filters, count):
    width = filters.shape[-1]
    total = jnp.zeros(extended.shape[:2] + (count, extended.shape[3]), jnp.float32)
    for tap in range(width):
        total = total + filters[:, None, None, :, tap] * extended[:, :, tap : tap + count]
    return total


def filter_terms(grads, extended, count, width):
    columns = []
    for tap in range(width):
        begin = width - 1 - tap
        columns.append(
            jnp.sum(grads * extended[:, :, begin : begin + count].astype(jnp.float32), axis=(1, 2))
        )
    return jnp.stack(columns, axis=-1)


def shards(inputs, key_panel, value_panel, short_filters, medium_filters, lengths, cotangent):
    seqs, count, local_width = inputs.shape
    channels = key_panel.shape[1]
    groups, taps = medium_filters.shape
    group_size = channels // groups
    short_width = short_filters.shape[-1]
    span = count + taps - 1
    gathered = (
        lax.all_gather(key_panel, "dp", axis=0, tiled=True),
        lax.all_gather(value_panel, "dp", axis=0, tiled=True),
    )
    panels = jnp.concatenate([gathered[0], gathered[1]], axis=1)
    features = lax.all_gather(inputs, "shard", axis=2, tiled=True)
    projected = jnp.dot(
        features.reshape(seqs * count, -1), panels, preferred_element_type=jnp.float32
    )
    paired = projected.astype(jnp.bfloat16).reshape(seqs, count, 2, channels).transpose(2, 0, 1, 3)
    head_rows = shifted(paired[:, :, count - (short_width - 1) :], "dp", 1)
    extended = jnp.concatenate([head_rows, paired], axis=2)
    smoothed = short_taps(extended, short_filters, count)
    product = (smoothed[0] * smoothed[1]).astype(jnp.bfloat16)
    before = shifted(product[:, count - (taps - 1) :], "dp", 1)
    product_ext = jnp.concatenate([before, product], axis=1).reshape(seqs, span, groups, group_size)
    forward_band = band(medium_filters[:, ::-1], count)
    response = jnp.einsum(
        "gtr,srgm->stgm",
        forward_band,
        product_ext.astype(jnp.float32),
        precision=lax.Precision.HIGHEST,
    ).reshape(seqs, count, channels)
    position = lax.axis_index("dp") * count + jnp.arange(count, dtype=jnp.int32)
    live = (position[None, :] < lengths[:, None])[:, :, None]
    mixed = jnp.where(live, response, 0.0).astype(jnp.bfloat16)
    upstream = jnp.where(live, cotangent, jnp.zeros_like(cotangent))
    after = shifted(upstream[:, : taps - 1], "dp", -1)
    upstream_ext = jnp.concatenate([upstream, after], axis=1).reshape(
        seqs, span, groups, group_size
    )
    backward_band = band(medium_filters, count)
    product_grad = jnp.einsum(
        "gtr,srgm->stgm",
        backward_band,
        upstream_ext.astype(jnp.float32),
        precision=lax.Precision.HIGHEST,
    ).reshape(seqs, count, channels)
    correlation = jnp.einsum(
        "stgm,srgm->gtr",
        upstream.reshape(seqs, count, groups, group_size),
        product_ext,
        preferred_element_type=jnp.float32,
    )
    medium_local = band_sums(correlation, count, taps)
    smooth_grad = jnp.stack([product_grad * smoothed[1], product_grad * smoothed[0]])
    short_local = filter_terms(smooth_grad, extended, count, short_width)
    ahead_rows = shifted(smooth_grad[:, :, : short_width - 1], "dp", -1)
    pair_grad = short_ahead(
        jnp.concatenate([smooth_grad, ahead_rows], axis=2), short_filters, count
    )
    short_grad, medium_grad = lax.psum((short_local, medium_local), "dp")
    outgoing = (
        pair_grad.astype(jnp.bfloat16).transpose(1, 2, 0, 3).reshape(seqs * count, 2 * channels)
    )
    flat_features = features.reshape(seqs * count, -1)
    grads = lax.psum_scatter(
        lax.dot_general(
            flat_features, outgoing, (((0,), (0,)), ((), ())), preferred_element_type=jnp.float32
        ).astype(jnp.bfloat16),
        "dp",
        scatter_dimension=0,
        tiled=True,
    ).astype(jnp.float32)
    key_grad = grads[:, :channels].astype(jnp.bfloat16)
    value_grad = grads[:, channels:].astype(jnp.bfloat16)
    return (mixed, key_grad, value_grad, short_grad, medium_grad)


def solution(mesh):
    return jax.shard_map(
        shards,
        mesh=mesh,
        in_specs=(
            P(None, "dp", "shard"),
            P("dp", "shard"),
            P("dp", "shard"),
            P(None, "shard", None),
            P("shard", None),
            P(),
            P(None, "dp", "shard"),
        ),
        out_specs=(
            P(None, "dp", "shard"),
            P("dp", "shard"),
            P("dp", "shard"),
            P(None, "shard", None),
            P("shard", None),
        ),
        check_vma=False,
    )
```

profile of v0, /device:TPU:2, one launch (start us, length us, event | category | flops | bytes accessed | tf_op | source)
XLA Modules:
  0.0 517.8 jit_solution(16801808159717984822)
XLA Ops:
  9.4 1.0 copy.29
  11.2 7.8 %collective-permute-start.2 = (bf16[2,127,128]{1,2,0:T(8,128)(2,1)S(1)}, bf16[2,127,128]{1,2,0:T(8,128)(2,1)S(1)}, u32[]{:S(2)}, u32[]{:S(2)}) collective-permute-start(bf16[2,127,128]{1,2,0:T(8,128)(2,1)S(1)} %slice.152), channel_id=1, source_target_pairs={{32,0},{64,32},{96,64},{128,96},{160,128},{192,160},{224,192},{256... | collective-permute-start | bytes 195080 | tf_op jit(solution)/shard_map/ppermute | solution.py:10
  19.0 1.4 slice_bitcast_fusion.6
  21.3 1.9 slice.153
  23.2 5.5 %reshape.111 = f32[8,256,383,1]{2,1,0,3:T(8,128)S(1)} reshape(f32[8,98048]{1,0:T(8,128)} %slice.153) | data formatting | bytes 6275072 | tf_op jit(solution)/shard_map/reshape | solution.py:18
  29.4 79.5 %all-gather.4.cloned.1.call-done = bf16[8192,128]{1,0:T(8,128)(2,1)} async-done(((bf16[512,128]{1,0:T(8,128)(2,1)}), bf16[8192,128]{1,0:T(8,128)(2,1)}) %all-gather.4.cloned.1.call-update) | async-done | bytes 2097168 | tf_op jit(solution)/shard_map/all_gather | solution.py:66
  108.9 90.8 %all-gather.6.cloned.1.call-done = bf16[8192,128]{1,0:T(8,128)(2,1)} async-done(((bf16[512,128]{1,0:T(8,128)(2,1)}), bf16[8192,128]{1,0:T(8,128)(2,1)}) %all-gather.6.cloned.1.call-update) | async-done | bytes 2097168 | tf_op jit(solution)/shard_map/all_gather | solution.py:67
  199.8 87.3 %all-gather.8.cloned.1.call-done = bf16[2,256,8192]{2,1,0:T(8,128)(2,1)} async-done(((bf16[2,256,256]{2,1,0:T(8,128)(2,1)}), bf16[2,256,8192]{2,1,0:T(8,128)(2,1)}) %all-gather.8.cloned.1.call-update) | async-done | bytes 8388624 | tf_op jit(solution)/shard_map/all_gather | solution.py:70
  287.1 7.7 %fusion.12 = bf16[512,256]{0,1:T(8,128)(2,1)} fusion(bf16[512,8192]{1,0:T(8,128)(2,1)} %bitcast.85, bf16[8192,128]{1,0:T(8,128)(2,1)} %all-gather.6.cloned.1.call-done, bf16[8192,128]{1,0:T(8,128)(2,1)} %all-gather.4.cloned.1.call-done), kind=kOutput, calls=%fused_computation.12 | convolution fusion | flops 2156003328 | bytes 12845056 | tf_op jit(solution)/shard_map/dot_general | solution.py:71
  294.8 1.0 reshape.99
  296.0 3.4 collective-permute-start
  299.4 2.6 fusion.18
  302.1 1.5 collective-permute-done
  303.6 0.9 fusion.26
  305.3 2.1 collective-permute-start.3
  307.4 7.4 %collective-permute-done.3 = f32[2,2,6,128]{2,3,1,0:T(8,128)S(1)} collective-permute-done((f32[2,2,6,128]{2,3,1,0:T(8,128)S(1)}, f32[2,2,6,128]{2,3,1,0:T(8,128)S(1)}, u32[]{:S(2)}, u32[]{:S(2)}) %collective-permute-start.3) | collective-permute-done | bytes 12320 | tf_op jit(solution)/shard_map/ppermute | solution.py:10
  314.8 1.1 fusion.50
  316.1 7.7 %fusion = bf16[8192,256]{0,1:T(8,128)(2,1)} fusion(bf16[512,8192]{1,0:T(8,128)(2,1)} %bitcast.86, bf16[64,8,2,128]{3,2,1,0:T(2,128)(2,1)S(1)} %bitcast.93), kind=kOutput, calls=%fused_computation.1 | convolution fusion | flops 2149580800 | bytes 12845056 | tf_op jit(solution)/shard_map/dot_general | solution.py:122
  324.8 1.9 slice.151
  326.7 5.5 %reshape.110 = f32[8,256,383,1]{2,1,0,3:T(8,128)S(1)} reshape(f32[8,98048]{1,0:T(8,128)} %slice.151) | data formatting | bytes 6275072 | tf_op jit(solution)/shard_map/reshape | solution.py:18
  332.2 0.9 slice.150
  333.2 6.4 %collective-permute-start.1 = (bf16[2,127,128]{1,2,0:T(8,128)(2,1)S(1)}, bf16[2,127,128]{1,2,0:T(8,128)(2,1)S(1)}, u32[]{:S(2)}, u32[]{:S(2)}) collective-permute-start(bf16[2,127,128]{1,2,0:T(8,128)(2,1)S(1)} %slice.150), channel_id=1, source_target_pairs={{0,32},{32,64},{64,96},{96,128},{128,160},{160,192},{192,224},{224... | collective-permute-start | bytes 195080 | tf_op jit(solution)/shard_map/ppermute | solution.py:10
  339.6 3.4 fusion.32
  343.1 1.0 pad_maximum_fusion.3
  344.1 2.3 convolution_bitcast_fusion
  346.5 5.2 %reshape.108 = f32[8,98048]{1,0:T(8,128)} reshape(f32[8,256,383]{2,1,0:T(8,128)} %convolution_bitcast_fusion) | data formatting | bytes 6275072 | tf_op jit(solution)/shard_map/reshape | solution.py:23
  351.7 3.8 concatenate.31
  355.5 2.2 reduce_sum.79
  357.8 1.7 fusion.15
  360.3 118.0 %all-reduce.3 = (f32[2,128,7]{1,0,2:T(2,128)}, f32[8,128]{1,0:T(8,128)}) all-reduce(f32[2,128,7]{1,0,2:T(2,128)S(1)} %constant_dynamic-update-slice_fusion, f32[8,128]{1,0:T(8,128)S(1)} %rev.7), channel_id=1, replica_groups=mesh['dp'=16,'shard'=32] {'dp'}, use_global_device_ids=true, to_apply=%region_8.9 | all-reduce | flops 2816 | bytes 22528 | tf_op jit(solution)/shard_map/psum | solution.py:116
  478.3 30.5 %reduce-scatter.2.cloned.1.call-done = bf16[512,256]{0,1:T(8,128)(2,1)} async-done(((bf16[8192,256]{0,1:T(8,128)(2,1)}), bf16[512,256]{0,1:T(8,128)(2,1)}) %reduce-scatter.2.cloned.1.call-update) | async-done | bytes 262160 | tf_op jit(solution)/shard_map/reduce_scatter | solution.py:121
  508.8 1.0 fusion.55
  (59 shorter events, 9.1 us)
Async XLA Ops:
  7.2 101.8 %all-gather.4.cloned.1.call-start = ((), (), s32[]{:S(2)}) async-start(), calls=%async_computation.1 | async-start | bytes 2228224 | tf_op jit(solution)/shard_map/all_gather | solution.py:66
  7.9 191.9 %all-gather.6.cloned.1.call-start = ((), (), s32[]{:S(2)}) async-start(), calls=%async_computation.2 | async-start | bytes 2228224 | tf_op jit(solution)/shard_map/all_gather | solution.py:67
  8.6 278.4 %all-gather.8.cloned.1.call-start = ((), (), s32[]{:S(2)}) async-start(), calls=%async_computation.3 | async-start | bytes 8650752 | tf_op jit(solution)/shard_map/all_gather | solution.py:70
  9.4 499.4 %reduce-scatter.2.cloned.1.call-start = ((), (), s32[]{:S(2)}) async-start(), calls=%async_computation.4 | async-start | bytes 4456448 | tf_op jit(solution)/shard_map/reduce_scatter | solution.py:121
  11.2 17.5 %collective-permute-start.2 = (bf16[2,127,128]{1,2,0:T(8,128)(2,1)S(1)}, bf16[2,127,128]{1,2,0:T(8,128)(2,1)S(1)}, u32[]{:S(2)}, u32[]{:S(2)}) collective-permute-start(bf16[2,127,128]{1,2,0:T(8,128)(2,1)S(1)} %slice.152), channel_id=1, source_target_pairs={{32,0},{64,32},{96,64},{128,96},{160,128},{192,160},{224,192},{256... | collective-permute-start | bytes 195080 | tf_op jit(solution)/shard_map/ppermute | solution.py:10
  295.8 7.8 %copy-start.2 = (bf16[2,256,2,128]{1,0,3,2:T(2,128)(2,1)}, bf16[2,256,2,128]{1,0,3,2:T(2,128)(2,1)S(1)}, u32[]{:S(2)}) copy-start(bf16[2,256,2,128]{1,0,3,2:T(2,128)(2,1)S(1)} %reshape.99) | copy-start | bytes 786436
  295.8 7.7 %copy-start.5 = (f32[2,128]{1,0:T(2,128)S(1)}, f32[2,128]{1,0:T(2,128)}, u32[]{:S(2)}) copy-start(f32[2,128]{1,0:T(2,128)} %get-tuple-element.42) | copy-start | bytes 3076
  295.8 7.7 %copy-start.6 = (f32[2,128]{1,0:T(2,128)S(1)}, f32[2,128]{1,0:T(2,128)}, u32[]{:S(2)}) copy-start(f32[2,128]{1,0:T(2,128)} %get-tuple-element.43) | copy-start | bytes 3076
  295.8 7.7 %copy-start.7 = (f32[2,128]{1,0:T(2,128)S(1)}, f32[2,128]{1,0:T(2,128)}, u32[]{:S(2)}) copy-start(f32[2,128]{1,0:T(2,128)} %get-tuple-element.44) | copy-start | bytes 3076
  295.9 7.7 %copy-start.8 = (f32[2,128]{1,0:T(2,128)S(1)}, f32[2,128]{1,0:T(2,128)}, u32[]{:S(2)}) copy-start(f32[2,128]{1,0:T(2,128)} %get-tuple-element.45) | copy-start | bytes 3076
  295.9 9.3 %copy-start.1 = (bf16[2,256,2,128]{1,3,0,2:T(8,128)(2,1)}, bf16[2,256,2,128]{1,3,0,2:T(8,128)(2,1)S(1)}, u32[]{:S(2)}) copy-start(bf16[2,256,2,128]{1,3,0,2:T(8,128)(2,1)S(1)} %copy.50) | copy-start | bytes 786436
  296.0 7.5 %collective-permute-start = (bf16[2,2,6,128]{2,3,1,0:T(8,128)(2,1)S(1)}, bf16[2,2,6,128]{2,3,1,0:T(8,128)(2,1)S(1)}, u32[]{:S(2)}, u32[]{:S(2)}) collective-permute-start(bf16[2,2,6,128]{2,3,1,0:T(8,128)(2,1)S(1)} %slice.137), channel_id=1, source_target_pairs={{0,32},{32,64},{64,96},{96,128},{128,160},{160,192},{192,224},{224... | collective-permute-start | bytes 18440 | tf_op jit(solution)/shard_map/ppermute | solution.py:10
  303.6 11.2 %copy-start.3 = (bf16[2,2,6,128]{2,3,1,0:T(8,128)(2,1)}, bf16[2,2,6,128]{2,3,1,0:T(8,128)(2,1)S(1)}, u32[]{:S(2)}) copy-start(bf16[2,2,6,128]{2,3,1,0:T(8,128)(2,1)S(1)} %collective-permute-done) | copy-start | bytes 18436
  305.2 9.6 %copy-start = (f32[1,2,256,128]{2,3,1,0:T(8,128)}, f32[1,2,256,128]{2,3,1,0:T(8,128)S(1)}, u32[]{:S(2)}) copy-start(f32[1,2,256,128]{2,3,1,0:T(8,128)S(1)} %get-tuple-element.35) | copy-start | bytes 786436
  305.3 9.5 %collective-permute-start.3 = (f32[2,2,6,128]{2,3,1,0:T(8,128)S(1)}, f32[2,2,6,128]{2,3,1,0:T(8,128)S(1)}, u32[]{:S(2)}, u32[]{:S(2)}) collective-permute-start(f32[2,2,6,128]{2,3,1,0:T(8,128)S(1)} %fusion.46), channel_id=1, source_target_pairs={{32,0},{64,32},{96,64},{128,96},{160,128},{192,160},{224,192},{256... | collective-permute-start | bytes 36872 | tf_op jit(solution)/shard_map/ppermute | solution.py:10
  323.8 0.7 copy-start.4
  333.2 9.9 %collective-permute-start.1 = (bf16[2,127,128]{1,2,0:T(8,128)(2,1)S(1)}, bf16[2,127,128]{1,2,0:T(8,128)(2,1)S(1)}, u32[]{:S(2)}, u32[]{:S(2)}) collective-permute-start(bf16[2,127,128]{1,2,0:T(8,128)(2,1)S(1)} %slice.150), channel_id=1, source_target_pairs={{0,32},{32,64},{64,96},{96,128},{128,160},{160,192},{192,224},{224... | collective-permute-start | bytes 195080 | tf_op jit(solution)/shard_map/ppermute | solution.py:10
Sparse Core Ops, SparseCore 0:
  11.0 97.9 all-gather.3
  111.9 87.7 all-gather.5
  201.8 85.1 all-gather.7
  324.0 184.7 reduce-scatter.1
where the time goes:
time: 519 us; the launch traced here: 518 us
  waiting for transfers between devices  299 us (58%)
  blocking collectives  118 us (23%)
  local copies, waits for them, and re-layouts  33.8 us (7%)
  matrix products  22.1 us (4%)
  starting transfers between devices  19.8 us (4%)
  between operations  14.1 us (3%)
  other arithmetic  10.9 us (2%)
    psum x1, blocking collectives, shards(): short_grad, medium_grad = lax.psum((short_local, medium_local), 'dp')  118 us
    all_gather x1, waiting for transfers between devices, shards(): lax.all_gather(value_panel, 'dp', axis=0, tiled=True)  90.8 us
    all_gather x1, waiting for transfers between devices, shards(): features = lax.all_gather(inputs, 'shard', axis=2, tiled=True)  87.3 us
    all_gather x1, waiting for transfers between devices, shards(): lax.all_gather(key_panel, 'dp', axis=0, tiled=True)  79.5 us
    reduce_scatter x1, waiting for transfers between devices, shards(): lax.psum_scatter(lax.dot_general(flat_features, outgoing, (((0,), (0,)),...  30.5 us
    ppermute x4, starting transfers between devices, shifted(): lax.ppermute(value, axis, [(source, source + steps) for source in range(f...  19.7 us
    reshape x2, local copies, waits for them, and re-layouts, band(): return tiled.reshape(groups, count, width)  11.1 us
  transfers between devices with their start and end apart: 8, of which 6 were waited for; matrix products, arithmetic and copies ran while one was open for 8% of the time, Pallas kernels for 0%

commit v1 on v0

--- a/solution.py
+++ b/solution.py
@@ -1,7 +1,17 @@
+import functools
 import jax
 import jax.numpy as jnp
 from jax import lax
 from jax.sharding import PartitionSpec as P
+
+
+def _point_goods(original, axis_id):
+    x_now = lax.all_to_all(jnp.stack([original] * lax.psum(1, axis_id), axis=0), axis_id, 0, 0)
+    outcome_arr = jnp.concatenate(x_now, axis=2)
+    return outcome_arr
+
+
+number_the_series_all = functools.partial(_point_goods, axis_id="shard")
 
 
 def shifted(value, axis, steps):
@@ -67,7 +77,7 @@
         lax.all_gather(value_panel, "dp", axis=0, tiled=True),
     )
     panels = jnp.concatenate([gathered[0], gathered[1]], axis=1)
-    features = lax.all_gather(inputs, "shard", axis=2, tiled=True)
+    features = number_the_series_all(inputs)
     projected = jnp.dot(
         features.reshape(seqs * count, -1), panels, preferred_element_type=jnp.float32
     )

time: 519 us -> 559 us (1.077)
  the two profiles are of different devices: /device:TPU:2 before, /device:TPU:24 now
where the time goes in v1:
time: 559 us; the launch traced here: 549 us
  waiting for transfers between devices  297 us (53%)
  blocking collectives  122 us (22%)
  local copies, waits for them, and re-layouts  64.1 us (11%)
  matrix products  22 us (4%)
  starting transfers between devices  18.6 us (3%)
  between operations  14.4 us (3%)
  other arithmetic  10.3 us (2%)
    all_to_all x1, waiting for transfers between devices, _point_goods(): lax.all_to_all(jnp.stack([original] * lax.psum(1, axis_id), axis=0), axis...  258 us
    psum x1, blocking collectives, shards(): short_grad, medium_grad = lax.psum((short_local, medium_local), 'dp')  122 us
    reduce_scatter x1, waiting for transfers between devices, shards(): lax.psum_scatter(lax.dot_general(flat_features, outgoing, (((0,), (0,)),...  28.6 us
    unnamed x37, local copies, waits for them, and re-layouts  19.4 us
    reshape x1, local copies, waits for them, and re-layouts, _point_goods(): outcome_arr = jnp.concatenate(x_now, axis=2)  11.4 us
  transfers between devices with their start and end apart: 8, of which 4 were waited for; matrix products, arithmetic and copies ran while one was open for 13% of the time, Pallas kernels for 0%

profile of v1, /device:TPU:24, one launch (start us, length us, event | category | flops | bytes accessed | tf_op | source)
XLA Modules:
  0.0 549.0 jit_solution(17187743497083070151)
XLA Ops:
  7.2 5.2 stack.20
  12.4 10.4 %all-to-all-start = ((bf16[32,2,256,256]{3,2,1,0:T(8,128)(2,1)}), bf16[32,2,256,256]{3,2,1,0:T(8,128)(2,1)}, u32[]{:S(2)}, u32[]{:S(2)}) async-start(bf16[32,2,256,256]{3,2,1,0:T(8,128)(2,1)} %stack.20), calls=%async_computation | async-start | bytes 16777216 | tf_op jit(solution)/shard_map/all_to_all | solution.py:9
  24.6 1.3 collective-permute-start.2
  26.7 1.8 slice.153
  28.5 5.5 %reshape.112 = f32[8,256,383,1]{2,1,0,3:T(8,128)S(1)} reshape(f32[8,98048]{1,0:T(8,128)} %slice.153) | data formatting | bytes 6275072 | tf_op jit(solution)/shard_map/reshape | solution.py:28
  34.8 258.1 %all-to-all-done = bf16[32,2,256,256]{3,2,1,0:T(8,128)(2,1)} async-done(((bf16[32,2,256,256]{3,2,1,0:T(8,128)(2,1)}), bf16[32,2,256,256]{3,2,1,0:T(8,128)(2,1)}, u32[]{:S(2)}, u32[]{:S(2)}) %all-to-all-start) | async-done | bytes 8388640 | tf_op jit(solution)/shard_map/all_to_all | solution.py:9
  292.8 11.4 %copy.36 = bf16[2,256,32,256]{3,2,1,0:T(8,128)(2,1)} copy(bf16[2,256,32,256]{3,1,0,2:T(8,128)(2,1)} %bitcast.1) | data formatting | bytes 16777216 | tf_op jit(solution)/shard_map/reshape | solution.py:10
  304.2 16.9 %copy.49 = bf16[64,8,32,256]{3,1,2,0:T(8,128)(2,1)} copy(bf16[64,8,32,256]{3,2,1,0:T(8,128)(2,1)} %bitcast.87) | data formatting | bytes 16777216
  321.1 7.8 %fusion.12 = bf16[512,256]{0,1:T(8,128)(2,1)} fusion(bf16[512,8192]{1,0:T(8,128)(2,1)} %bitcast.85, bf16[8192,128]{1,0:T(8,128)(2,1)} %all-gather.5.cloned.1.call-done, bf16[8192,128]{1,0:T(8,128)(2,1)} %all-gather.3.cloned.1.call-done), kind=kOutput, calls=%fused_computation.12 | convolution fusion | flops 2156003328 | bytes 12845056 | tf_op jit(solution)/shard_map/dot_general | solution.py:81
  328.9 1.0 reshape.100
  330.1 1.6 collective-permute-start
  331.7 2.6 fusion.18
  334.8 0.9 fusion.26
  336.4 1.3 collective-permute-start.3
  337.7 9.0 %collective-permute-done.3 = f32[2,2,6,128]{2,3,1,0:T(8,128)S(1)} collective-permute-done((f32[2,2,6,128]{2,3,1,0:T(8,128)S(1)}, f32[2,2,6,128]{2,3,1,0:T(8,128)S(1)}, u32[]{:S(2)}, u32[]{:S(2)}) %collective-permute-start.3) | collective-permute-done | bytes 12320 | tf_op jit(solution)/shard_map/ppermute | solution.py:20
  346.8 1.1 fusion.50
  348.1 7.7 %fusion = bf16[8192,256]{0,1:T(8,128)(2,1)} fusion(bf16[512,8192]{1,0:T(8,128)(2,1)} %bitcast.86, bf16[64,8,2,128]{3,2,1,0:T(2,128)(2,1)S(1)} %bitcast.97), kind=kOutput, calls=%fused_computation.1 | convolution fusion | flops 2149580800 | bytes 12845056 | tf_op jit(solution)/shard_map/dot_general | solution.py:132
  356.1 1.8 slice.151
  358.0 5.5 %reshape.111 = f32[8,256,383,1]{2,1,0,3:T(8,128)S(1)} reshape(f32[8,98048]{1,0:T(8,128)} %slice.151) | data formatting | bytes 6275072 | tf_op jit(solution)/shard_map/reshape | solution.py:28
  363.5 0.9 slice.150
  364.4 3.9 collective-permute-start.1
  368.3 3.4 fusion.32
  371.8 1.0 pad_maximum_fusion.3
  372.9 2.3 convolution_bitcast_fusion
  375.1 5.2 reshape.109
  380.4 3.7 concatenate.31
  384.1 2.2 reduce_sum.79
  386.4 1.7 fusion.15
  388.1 0.8 copy.44
  388.9 122.2 %all-reduce.3 = (f32[2,128,7]{1,0,2:T(2,128)}, f32[8,128]{1,0:T(8,128)}) all-reduce(f32[2,128,7]{1,0,2:T(2,128)S(1)} %constant_dynamic-update-slice_fusion, f32[8,128]{1,0:T(8,128)S(1)} %rev.7), channel_id=1, replica_groups=mesh['dp'=16,'shard'=32] {'dp'}, use_global_device_ids=true, to_apply=%region_8.9 | all-reduce | flops 2816 | bytes 22528 | tf_op jit(solution)/shard_map/psum | solution.py:126
  511.1 28.6 %reduce-scatter.2.cloned.1.call-done = bf16[512,256]{0,1:T(8,128)(2,1)} async-done(((bf16[8192,256]{0,1:T(8,128)(2,1)}), bf16[512,256]{0,1:T(8,128)(2,1)}) %reduce-scatter.2.cloned.1.call-update) | async-done | bytes 262160 | tf_op jit(solution)/shard_map/reduce_scatter | solution.py:131
  539.7 1.0 fusion.55
  (69 shorter events, 6.7 us)
Async XLA Ops:
  12.4 12.0 %copy-start.4 = (bf16[2,256,128]{2,1,0:T(8,128)(2,1)S(1)}, bf16[2,256,128]{2,1,0:T(8,128)(2,1)}, u32[]{:S(2)}) copy-start(bf16[2,256,128]{2,1,0:T(8,128)(2,1)} %param.13) | copy-start | bytes 393220
  12.4 12.1 %copy-start.12 = (s32[2]{0:T(128)S(1)}, s32[2]{0:T(128)}, u32[]{:S(2)}) copy-start(s32[2]{0:T(128)} %param.12) | copy-start | bytes 28
  12.4 13.5 %copy-start.11 = (f32[2,128,7]{1,0,2:T(2,128)S(1)}, f32[2,128,7]{1,0,2:T(2,128)}, u32[]{:S(2)}) copy-start(f32[2,128,7]{1,0,2:T(2,128)} %param.10) | copy-start | bytes 21508
  12.4 14.1 %copy-start.5 = (f32[8,128]{1,0:T(8,128)S(1)}, f32[8,128]{1,0:T(8,128)}, u32[]{:S(2)}) copy-start(f32[8,128]{1,0:T(8,128)} %param.11) | copy-start | bytes 12292
  12.4 280.5 %all-to-all-start = ((bf16[32,2,256,256]{3,2,1,0:T(8,128)(2,1)}), bf16[32,2,256,256]{3,2,1,0:T(8,128)(2,1)}, u32[]{:S(2)}, u32[]{:S(2)}) async-start(bf16[32,2,256,256]{3,2,1,0:T(8,128)(2,1)} %stack.20), calls=%async_computation | async-start | bytes 16777216 | tf_op jit(solution)/shard_map/all_to_all | solution.py:9
  22.8 298.3 %all-gather.3.cloned.1.call-start = ((), (), s32[]{:S(2)}) async-start(), calls=%async_computation.2 | async-start | bytes 2228224 | tf_op jit(solution)/shard_map/all_gather | solution.py:76
  23.5 297.6 %all-gather.5.cloned.1.call-start = ((), (), s32[]{:S(2)}) async-start(), calls=%async_computation.3 | async-start | bytes 2228224 | tf_op jit(solution)/shard_map/all_gather | solution.py:77
  24.3 515.4 %reduce-scatter.2.cloned.1.call-start = ((), (), s32[]{:S(2)}) async-start(), calls=%async_computation.4 | async-start | bytes 4456448 | tf_op jit(solution)/shard_map/reduce_scatter | solution.py:131
  24.6 9.5 %collective-permute-start.2 = (bf16[2,127,128]{1,2,0:T(8,128)(2,1)S(1)}, bf16[2,127,128]{1,2,0:T(8,128)(2,1)S(1)}, u32[]{:S(2)}, u32[]{:S(2)}) collective-permute-start(bf16[2,127,128]{1,2,0:T(8,128)(2,1)S(1)} %slice.152), channel_id=1, source_target_pairs={{32,0},{64,32},{96,64},{128,96},{160,128},{192,160},{224,192},{256... | collective-permute-start | bytes 195080 | tf_op jit(solution)/shard_map/ppermute | solution.py:20
  329.9 4.8 copy-start.2
  329.9 4.8 copy-start.6
  329.9 4.8 copy-start.7
  329.9 4.8 copy-start.8
  329.9 4.8 copy-start.9
  330.0 4.8 copy-start.10
  330.0 6.4 %copy-start.1 = (bf16[2,256,2,128]{1,3,0,2:T(8,128)(2,1)}, bf16[2,256,2,128]{1,3,0,2:T(8,128)(2,1)S(1)}, u32[]{:S(2)}) copy-start(bf16[2,256,2,128]{1,3,0,2:T(8,128)(2,1)S(1)} %copy.62) | copy-start | bytes 786436
  330.1 4.6 collective-permute-start
  334.7 12.0 %copy-start.3 = (bf16[2,2,6,128]{2,3,1,0:T(8,128)(2,1)}, bf16[2,2,6,128]{2,3,1,0:T(8,128)(2,1)S(1)}, u32[]{:S(2)}) copy-start(bf16[2,2,6,128]{2,3,1,0:T(8,128)(2,1)S(1)} %collective-permute-done) | copy-start | bytes 18436
  336.4 10.4 %copy-start = (f32[1,2,256,128]{2,3,1,0:T(8,128)}, f32[1,2,256,128]{2,3,1,0:T(8,128)S(1)}, u32[]{:S(2)}) copy-start(f32[1,2,256,128]{2,3,1,0:T(8,128)S(1)} %get-tuple-element.40) | copy-start | bytes 786436
  336.4 10.3 %collective-permute-start.3 = (f32[2,2,6,128]{2,3,1,0:T(8,128)S(1)}, f32[2,2,6,128]{2,3,1,0:T(8,128)S(1)}, u32[]{:S(2)}, u32[]{:S(2)}) collective-permute-start(f32[2,2,6,128]{2,3,1,0:T(8,128)S(1)} %fusion.46), channel_id=1, source_target_pairs={{32,0},{64,32},{96,64},{128,96},{160,128},{192,160},{224,192},{256... | collective-permute-start | bytes 36872 | tf_op jit(solution)/shard_map/ppermute | solution.py:20
  364.4 7.4 %collective-permute-start.1 = (bf16[2,127,128]{1,2,0:T(8,128)(2,1)S(1)}, bf16[2,127,128]{1,2,0:T(8,128)(2,1)S(1)}, u32[]{:S(2)}, u32[]{:S(2)}) collective-permute-start(bf16[2,127,128]{1,2,0:T(8,128)(2,1)S(1)} %slice.150), channel_id=1, source_target_pairs={{0,32},{32,64},{64,96},{96,128},{128,160},{160,192},{192,224},{224... | collective-permute-start | bytes 195080 | tf_op jit(solution)/shard_map/ppermute | solution.py:20
Sparse Core Ops, SparseCore 0:
  26.6 99.5 all-gather.2
  129.2 129.6 all-gather.4
  355.9 183.7 reduce-scatter.1
